TPU v7x, 32 devices: a whole 2x2x4 slice. The times are simulated.
32 devices in a mesh: inst: 4 (over z), shard: 8 (over y, x, core).
Axes of the slice: x: 2, y: 2, z: 4, core: 2. Of those that a mesh axis runs over, the one named last changes fastest.
Arguments:
- master_old: float32 [4, 16, 65536], P('inst', 'shard'), may hold values from -3 to 3
- first_old: float32 [4, 16, 65536], P('inst', 'shard'), may hold values from -2 to 2
- second_old: float32 [4, 16, 65536], P('inst', 'shard'), may hold values from 0.01 to 1
- healthy: int32 [8], replicated, may hold values from 0 to 3
- slice_table: int32 [16], replicated, may hold values from 0 to 15, as said below
Outputs:
- master_new: float32 [4, 16, 65536], P('inst', 'shard')
- first_new: float32 [4, 16, 65536], P('inst', 'shard')
- second_new: float32 [4, 16, 65536], P('inst', 'shard')
- params_half: bfloat16 [4, 16, 65536], P('inst', 'shard')
- checksum: float32 [4, 2], P('inst')
Inputs may be any that keep to these rules, and one draw needn't show every extreme that they name: slice_table[k] = (k + slice_table[0]) mod 16 for every k, with slice_table[0] odd and at least 3.
All inputs are finite; a program needn't handle non-finite values.
Results may differ from a plain program's by a relative error of at most 0.001.
Values sent between devices are 32-bit elements; how exact they have to be, the bound alone decides.
No kernel may reach another device: no remote copies, remote signals or barrier semaphores. Data moves between devices by JAX's collectives and lax.ppermute only.
A program may use at most 64 MiB of HBM per device.

v0:
```python
import jax
import jax.numpy as jnp
from jax import lax
from jax.sharding import PartitionSpec as P


def passed_along(value, axis, steps):
    count = lax.axis_size(axis)
    pairs = [(source, (source + steps) % count) for source in range(count)]
    return lax.ppermute(value, axis, pairs)


def from_root(block, axis, owner):
    block = jnp.where(lax.axis_index(axis) == owner, block, jnp.zeros_like(block))
    return lax.psum(block, axis)


def position_keys(flat_rows, columns):
    residue = flat_rows * (columns % 101) % 101
    offsets = jnp.arange(columns, dtype=jnp.int32)
    cycled = (residue[:, None] + offsets[None, :]) % 101
    return (cycled * 37 % 101 + 1).astype(jnp.float32) / 101.0


def weighted(master, first_moment, second, flat_rows):
    weights = position_keys(flat_rows, master.shape[2])
    combined = master[0] + first_moment[0] + second[0]
    return jnp.stack([jnp.sum(combined * weights), jnp.sum(master[0] * weights)])


def grand_total(partial_value):
    return lax.psum(partial_value, "shard")


def join_parts(pieces):
    return (
        lax.all_gather(pieces[0], "inst", axis=2, tiled=True),
        lax.all_gather(pieces[1], "inst", axis=2, tiled=True),
        lax.all_gather(pieces[2], "inst", axis=2, tiled=True),
    )


def reorder(arrays, rotation, owners):
    for bit_level in range((owners - 1).bit_length()):
        shifted = passed_along((arrays[0], arrays[1], arrays[2]), "shard", 1 << bit_level)
        chosen = rotation >> bit_level & 1 == 1
        arrays = tuple(
            (
                jnp.where(chosen, shifted_one, current)
                for shifted_one, current in zip(shifted, arrays)
            )
        )
    carried = passed_along((arrays[0][:, 1:2], arrays[1][:, 1:2], arrays[2][:, 1:2]), "shard", 1)
    return tuple(
        (
            jnp.concatenate([carried_one, current[:, 0:1]], axis=1)
            for carried_one, current in zip(carried, arrays)
        )
    )


def on_device(master_old, first_old, second_old, healthy, slice_table):
    source_index = lax.dynamic_index_in_dim(healthy, lax.axis_index("shard"), 0, keepdims=False)
    owners = lax.axis_size("shard")
    instances = lax.axis_size("inst")
    columns = master_old.shape[2]
    part_len = columns // instances
    normalizer = 1.0 / (2.0 * columns)
    rotation = slice_table[0] // 2
    master, first_moment, second = (
        from_root(master_old, "inst", source_index),
        from_root(first_old, "inst", source_index),
        from_root(second_old, "inst", source_index),
    )
    offset_start = lax.axis_index("inst") * part_len
    pieces = tuple(
        (
            lax.dynamic_slice_in_dim(stacked, offset_start, part_len, 2)
            for stacked in (master, first_moment, second)
        )
    )
    pieces = reorder(pieces, rotation, owners)
    master, first_moment, second = join_parts(pieces)
    new_rows = 2 * lax.axis_index("shard") + jnp.arange(2, dtype=jnp.int32)
    checksum = grand_total(weighted(master, first_moment, second, new_rows))
    checksum = jnp.reshape(checksum * normalizer, (1, 2))
    return (master, first_moment, second, master.astype(jnp.bfloat16), checksum)


def solution(mesh):
    placed = (
        P("inst", "shard", None),
        P("inst", "shard", None),
        P("inst", "shard", None),
        P(),
        P(),
    )
    return jax.shard_map(
        on_device,
        mesh=mesh,
        in_specs=placed,
        out_specs=(
            P("inst", "shard", None),
            P("inst", "shard", None),
            P("inst", "shard", None),
            P("inst", "shard", None),
            P("inst", None),
        ),
        check_vma=False,
    )
```

profile of v0, /device:TPU:0, one launch (start us, length us, event | category | flops | bytes accessed | tf_op | source)
XLA Modules:
  0.0 187.4 jit_solution(15723886663687752897)
XLA Ops:
  7.2 0.0 all-reduce.3.cloned.1.call-start
  7.2 0.6 copy-done.4
  7.9 0.6 dynamic_slice.13
  9.1 0.0 copy-start
  9.1 0.0 copy-start.1
  9.1 1.0 broadcast_select_fusion.2
  10.2 0.2 copy-done.1
  10.4 1.5 broadcast_select_fusion
  11.9 0.0 all-reduce.3.cloned.1.call-update
  11.9 0.0 copy-start.3
  12.0 0.6 copy-done.3
  12.8 71.1 %all-reduce.3.cloned.1.call-done = (f32[1,2,65536]{2,1,0:T(2,128)}, f32[1,2,65536]{2,1,0:T(2,128)}, f32[1,2,65536]{2,1,0:T(2,128)}) async-done(((f32[1,2,65536]{2,1,0:T(2,128)}, f32[1,2,65536]{2,1,0:T(2,128)}, f32[1,2,65536]{2,1,0:T(2,128)}), (f32[1,2,65536]{2,1,0:T(2,128)}, f32[1,2,65536]{2,1,0:T(2,128)}, f32[1,2,65536]{2,1,0:T(2,128)})) %all-reduce.3.cloned.1.call-update) | async-done | bytes 1572880 | tf_op jit(solution)/shard_map/psum | solution.py:15
  83.9 1.0 constant_dynamic-slice_fusion
  84.9 0.1 collective-permute-start.8
  84.9 0.9 constant_dynamic-slice_fusion.1
  85.9 1.6 collective-permute-start.4
  87.5 0.1 collective-permute-start
  87.6 2.6 %collective-permute-done.8 = f32[1,2,16384]{2,1,0:T(2,128)S(1)} collective-permute-done((f32[1,2,16384]{2,1,0:T(2,128)S(1)}, f32[1,2,16384]{2,1,0:T(2,128)S(1)}, u32[]{:S(2)}, u32[]{:S(2)}) %collective-permute-start.8) | collective-permute-done | bytes 131104 | tf_op jit(solution)/shard_map/ppermute | solution.py:10
  90.2 1.0 broadcast_select_fusion.3
  91.2 0.6 collective-permute-start.9
  91.8 0.0 collective-permute-done.4
  91.8 1.0 broadcast_select_fusion.4
  92.8 2.4 %collective-permute-start.5 = (f32[1,2,16384]{2,1,0:T(2,128)S(1)}, f32[1,2,16384]{2,1,0:T(2,128)S(1)}, u32[]{:S(2)}, u32[]{:S(2)}) collective-permute-start(f32[1,2,16384]{2,1,0:T(2,128)S(1)} %broadcast_select_fusion.4), channel_id=1, source_target_pairs={{0,2},{1,3},{2,4},{3,5},{4,6},{5,7},{6,0},{7,1},{8,10},{9,11},{10,... | collective-permute-start | bytes 393224 | tf_op jit(solution)/shard_map/ppermute | solution.py:10
  95.2 0.0 collective-permute-done
  95.2 0.1 broadcast_select_fusion.5
  95.3 0.6 collective-permute-start.1
  95.9 2.5 %collective-permute-done.9 = f32[1,2,16384]{2,1,0:T(2,128)S(1)} collective-permute-done((f32[1,2,16384]{2,1,0:T(2,128)S(1)}, f32[1,2,16384]{2,1,0:T(2,128)S(1)}, u32[]{:S(2)}, u32[]{:S(2)}) %collective-permute-start.9) | collective-permute-done | bytes 131104 | tf_op jit(solution)/shard_map/ppermute | solution.py:10
  98.4 0.1 broadcast_select_fusion.6
  98.5 1.7 collective-permute-start.10
  100.2 1.0 collective-permute-done.5
  101.3 0.1 broadcast_select_fusion.7
  101.3 1.0 collective-permute-start.6
  102.3 0.5 collective-permute-done.1
  102.8 0.1 broadcast_select_fusion.8
  102.9 0.8 collective-permute-start.2
  103.7 1.9 %collective-permute-done.10 = f32[1,2,16384]{2,1,0:T(2,128)S(1)} collective-permute-done((f32[1,2,16384]{2,1,0:T(2,128)S(1)}, f32[1,2,16384]{2,1,0:T(2,128)S(1)}, u32[]{:S(2)}, u32[]{:S(2)}) %collective-permute-start.10) | collective-permute-done | bytes 131104 | tf_op jit(solution)/shard_map/ppermute | solution.py:10
  105.6 0.1 broadcast_select_fusion.9
  105.7 0.1 fusion.8
  105.8 0.1 collective-permute-start.11
  105.9 2.6 %collective-permute-done.6 = f32[1,2,16384]{2,1,0:T(2,128)S(1)} collective-permute-done((f32[1,2,16384]{2,1,0:T(2,128)S(1)}, f32[1,2,16384]{2,1,0:T(2,128)S(1)}, u32[]{:S(2)}, u32[]{:S(2)}) %collective-permute-start.6) | collective-permute-done | bytes 131104 | tf_op jit(solution)/shard_map/ppermute | solution.py:10
  108.4 0.1 broadcast_select_fusion.10
  108.5 0.1 fusion.9
  108.6 0.1 collective-permute-start.7
  108.7 3.2 %collective-permute-done.2 = f32[1,2,16384]{2,1,0:T(2,128)S(1)} collective-permute-done((f32[1,2,16384]{2,1,0:T(2,128)S(1)}, f32[1,2,16384]{2,1,0:T(2,128)S(1)}, u32[]{:S(2)}, u32[]{:S(2)}) %collective-permute-start.2) | collective-permute-done | bytes 131104 | tf_op jit(solution)/shard_map/ppermute | solution.py:10
  111.9 0.1 broadcast_select_fusion.11
  111.9 0.1 fusion.10
  112.0 0.1 collective-permute-start.3
  112.1 0.0 collective-permute-done.11
  112.1 0.1 pad_maximum_fusion.2
  112.2 16.1 %all_gather.11 = f32[1,2,65536]{2,1,0:T(2,128)S(1)} all-gather(f32[1,2,16384]{2,1,0:T(2,128)S(1)} %pad_maximum_fusion.2), channel_id=1, replica_groups=mesh['inst'=4,'shard'=8] {'inst'}, dimensions={2}, use_global_device_ids=true | all-gather | bytes 655360 | tf_op jit(solution)/shard_map/all_gather | solution.py:39
  128.3 0.0 collective-permute-done.7
  128.3 0.1 pad_maximum_fusion.1
  128.5 15.8 %all_gather.10 = f32[1,2,65536]{2,1,0:T(2,128)S(1)} all-gather(f32[1,2,16384]{2,1,0:T(2,128)S(1)} %pad_maximum_fusion.1), channel_id=1, replica_groups=mesh['inst'=4,'shard'=8] {'inst'}, dimensions={2}, use_global_device_ids=true | all-gather | bytes 655360 | tf_op jit(solution)/shard_map/all_gather | solution.py:38
  144.2 0.0 collective-permute-done.3
  144.2 0.1 pad_maximum_fusion
  144.4 15.0 %all_gather.9 = f32[1,2,65536]{2,1,0:T(2,128)S(1)} all-gather(f32[1,2,16384]{2,1,0:T(2,128)S(1)} %pad_maximum_fusion), channel_id=1, replica_groups=mesh['inst'=4,'shard'=8] {'inst'}, dimensions={2}, use_global_device_ids=true | all-gather | bytes 655360 | tf_op jit(solution)/shard_map/all_gather | solution.py:37
  159.3 4.3 %fusion.6 = (f32[]{:T(128)}, f32[]{:T(128)}) fusion(f32[1,2,65536]{2,1,0:T(2,128)S(1)} %all_gather.11, f32[1,2,65536]{2,1,0:T(2,128)S(1)} %all_gather.10, f32[1,2,65536]{2,1,0:T(2,128)S(1)} %all_gather.9, s32[2]{0:T(128)S(1)} %and_select_fusion.2), kind=kLoop, calls=%fused_computation.9 | loop fusion | flops 3014654 | bytes 1572880 | tf_op jit(solution)/shard_map/reduce_sum | solution.py:28
  163.6 1.4 pad_maximum_fusion.3
  165.0 0.9 convert_element_type.6
  165.9 11.8 %psum.31 = f32[2]{0:T(128)S(1)} all-reduce(f32[2]{0:T(128)S(1)} %pad_maximum_fusion.3), channel_id=1, replica_groups=mesh['inst'=4,'shard'=8] {'shard'}, use_global_device_ids=true, to_apply=%region_5.6 | all-reduce | flops 2 | bytes 16 | tf_op jit(solution)/shard_map/psum | solution.py:32
  177.7 0.5 multiply_bitcast_fusion
  178.2 0.8 copy.16
  179.0 0.8 copy.17
  179.8 0.8 copy.18
  (6 shorter events, 0.0 us)
Async XLA Ops:
  7.2 76.7 %all-reduce.3.cloned.1.call-start = ((), (), s32[]{:S(2)}) async-start(), calls=%async_computation | async-start | bytes 3145728 | tf_op jit(solution)/shard_map/psum | solution.py:15
  7.2 0.7 copy-start.4
  9.1 1.1 copy-start
  9.1 1.3 copy-start.1
  11.9 0.7 copy-start.3
  83.9 3.6 %copy-start.2 = (f32[1,2,65536]{2,1,0:T(2,128)S(1)}, f32[1,2,65536]{2,1,0:T(2,128)}, u32[]{:S(2)}) copy-start(f32[1,2,65536]{2,1,0:T(2,128)} %get-tuple-element.7) | copy-start | bytes 1572868
  84.9 5.3 %collective-permute-start.8 = (f32[1,2,16384]{2,1,0:T(2,128)S(1)}, f32[1,2,16384]{2,1,0:T(2,128)S(1)}, u32[]{:S(2)}, u32[]{:S(2)}) collective-permute-start(f32[1,2,16384]{2,1,0:T(2,128)S(1)} %constant_dynamic-slice_fusion), channel_id=1, source_target_pairs={{0,1},{1,2},{2,3},{3,4},{4,5},{5,6},{6,7},{7,0},{8,9},{9,10},{10,1... | collective-permute-start | bytes 393224 | tf_op jit(solution)/shard_map/ppermute | solution.py:10
  85.9 6.0 %collective-permute-start.4 = (f32[1,2,16384]{2,1,0:T(2,128)S(1)}, f32[1,2,16384]{2,1,0:T(2,128)S(1)}, u32[]{:S(2)}, u32[]{:S(2)}) collective-permute-start(f32[1,2,16384]{2,1,0:T(2,128)S(1)} %constant_dynamic-slice_fusion.1), channel_id=1, source_target_pairs={{0,1},{1,2},{2,3},{3,4},{4,5},{5,6},{6,7},{7,0},{8,9},{9,10},{10,1... | collective-permute-start | bytes 393224 | tf_op jit(solution)/shard_map/ppermute | solution.py:10
  87.5 7.7 %collective-permute-start = (f32[1,2,16384]{2,1,0:T(2,128)S(1)}, f32[1,2,16384]{2,1,0:T(2,128)S(1)}, u32[]{:S(2)}, u32[]{:S(2)}) collective-permute-start(f32[1,2,16384]{2,1,0:T(2,128)S(1)} %constant_dynamic-slice_fusion.2), channel_id=1, source_target_pairs={{0,1},{1,2},{2,3},{3,4},{4,5},{5,6},{6,7},{7,0},{8,9},{9,10},{10,1... | collective-permute-start | bytes 393224 | tf_op jit(solution)/shard_map/ppermute | solution.py:10
  91.2 7.2 %collective-permute-start.9 = (f32[1,2,16384]{2,1,0:T(2,128)S(1)}, f32[1,2,16384]{2,1,0:T(2,128)S(1)}, u32[]{:S(2)}, u32[]{:S(2)}) collective-permute-start(f32[1,2,16384]{2,1,0:T(2,128)S(1)} %broadcast_select_fusion.3), channel_id=1, source_target_pairs={{0,2},{1,3},{2,4},{3,5},{4,6},{5,7},{6,0},{7,1},{8,10},{9,11},{10,... | collective-permute-start | bytes 393224 | tf_op jit(solution)/shard_map/ppermute | solution.py:10
  92.8 8.5 %collective-permute-start.5 = (f32[1,2,16384]{2,1,0:T(2,128)S(1)}, f32[1,2,16384]{2,1,0:T(2,128)S(1)}, u32[]{:S(2)}, u32[]{:S(2)}) collective-permute-start(f32[1,2,16384]{2,1,0:T(2,128)S(1)} %broadcast_select_fusion.4), channel_id=1, source_target_pairs={{0,2},{1,3},{2,4},{3,5},{4,6},{5,7},{6,0},{7,1},{8,10},{9,11},{10,... | collective-permute-start | bytes 393224 | tf_op jit(solution)/shard_map/ppermute | solution.py:10
  95.3 7.5 %collective-permute-start.1 = (f32[1,2,16384]{2,1,0:T(2,128)S(1)}, f32[1,2,16384]{2,1,0:T(2,128)S(1)}, u32[]{:S(2)}, u32[]{:S(2)}) collective-permute-start(f32[1,2,16384]{2,1,0:T(2,128)S(1)} %broadcast_select_fusion.5), channel_id=1, source_target_pairs={{0,2},{1,3},{2,4},{3,5},{4,6},{5,7},{6,0},{7,1},{8,10},{9,11},{10,... | collective-permute-start | bytes 393224 | tf_op jit(solution)/shard_map/ppermute | solution.py:10
  98.5 7.1 %collective-permute-start.10 = (f32[1,2,16384]{2,1,0:T(2,128)S(1)}, f32[1,2,16384]{2,1,0:T(2,128)S(1)}, u32[]{:S(2)}, u32[]{:S(2)}) collective-permute-start(f32[1,2,16384]{2,1,0:T(2,128)S(1)} %broadcast_select_fusion.6), channel_id=1, source_target_pairs={{0,4},{1,5},{2,6},{3,7},{4,0},{5,1},{6,2},{7,3},{8,12},{9,13},{10,... | collective-permute-start | bytes 393224 | tf_op jit(solution)/shard_map/ppermute | solution.py:10
  101.3 7.1 %collective-permute-start.6 = (f32[1,2,16384]{2,1,0:T(2,128)S(1)}, f32[1,2,16384]{2,1,0:T(2,128)S(1)}, u32[]{:S(2)}, u32[]{:S(2)}) collective-permute-start(f32[1,2,16384]{2,1,0:T(2,128)S(1)} %broadcast_select_fusion.7), channel_id=1, source_target_pairs={{0,4},{1,5},{2,6},{3,7},{4,0},{5,1},{6,2},{7,3},{8,12},{9,13},{10,... | collective-permute-start | bytes 393224 | tf_op jit(solution)/shard_map/ppermute | solution.py:10
  102.9 9.0 %collective-permute-start.2 = (f32[1,2,16384]{2,1,0:T(2,128)S(1)}, f32[1,2,16384]{2,1,0:T(2,128)S(1)}, u32[]{:S(2)}, u32[]{:S(2)}) collective-permute-start(f32[1,2,16384]{2,1,0:T(2,128)S(1)} %broadcast_select_fusion.8), channel_id=1, source_target_pairs={{0,4},{1,5},{2,6},{3,7},{4,0},{5,1},{6,2},{7,3},{8,12},{9,13},{10,... | collective-permute-start | bytes 393224 | tf_op jit(solution)/shard_map/ppermute | solution.py:10
  105.8 6.3 %collective-permute-start.11 = (f32[1,1,16384]{2,1,0:T(1,128)S(1)}, f32[1,1,16384]{2,1,0:T(1,128)S(1)}, u32[]{:S(2)}, u32[]{:S(2)}) collective-permute-start(f32[1,1,16384]{2,1,0:T(1,128)S(1)} %get-tuple-element.10), channel_id=1, source_target_pairs={{0,1},{1,2},{2,3},{3,4},{4,5},{5,6},{6,7},{7,0},{8,9},{9,10},{10,1... | collective-permute-start | bytes 196616 | tf_op jit(solution)/shard_map/ppermute | solution.py:10
  108.6 19.7 %collective-permute-start.7 = (f32[1,1,16384]{2,1,0:T(1,128)S(1)}, f32[1,1,16384]{2,1,0:T(1,128)S(1)}, u32[]{:S(2)}, u32[]{:S(2)}) collective-permute-start(f32[1,1,16384]{2,1,0:T(1,128)S(1)} %get-tuple-element.12), channel_id=1, source_target_pairs={{0,1},{1,2},{2,3},{3,4},{4,5},{5,6},{6,7},{7,0},{8,9},{9,10},{10,1... | collective-permute-start | bytes 196616 | tf_op jit(solution)/shard_map/ppermute | solution.py:10
  112.0 32.2 %collective-permute-start.3 = (f32[1,1,16384]{2,1,0:T(1,128)S(1)}, f32[1,1,16384]{2,1,0:T(1,128)S(1)}, u32[]{:S(2)}, u32[]{:S(2)}) collective-permute-start(f32[1,1,16384]{2,1,0:T(1,128)S(1)} %get-tuple-element.14), channel_id=1, source_target_pairs={{0,1},{1,2},{2,3},{3,4},{4,5},{5,6},{6,7},{7,0},{8,9},{9,10},{10,1... | collective-permute-start | bytes 196616 | tf_op jit(solution)/shard_map/ppermute | solution.py:10
Sparse Core Ops, SparseCore 0:
  12.1 71.7 all-reduce.2
where the time goes:
time: 188 us; the launch traced here: 187 us
  waiting for transfers between devices  85.5 us (45%)
  blocking collectives  58.6 us (31%)
  between operations  15 us (8%)
  other arithmetic  12.4 us (7%)
  starting transfers between devices  9.11 us (5%)
  local copies, waits for them, and re-layouts  6.73 us (4%)
    psum x1, waiting for transfers between devices, from_root(): return lax.psum(block, axis)  71.1 us
    all_gather x1, blocking collectives, join_parts(): lax.all_gather(pieces[2], 'inst', axis=2, tiled=True)  16.1 us
    all_gather x1, blocking collectives, join_parts(): lax.all_gather(pieces[1], 'inst', axis=2, tiled=True)  15.8 us
    all_gather x1, blocking collectives, join_parts(): lax.all_gather(pieces[0], 'inst', axis=2, tiled=True)  15 us
    ppermute x12, waiting for transfers between devices, passed_along(): return lax.ppermute(value, axis, pairs)  14.4 us
    psum x1, blocking collectives, grand_total(): return lax.psum(partial_value, 'shard')  11.8 us
    ppermute x12, starting transfers between devices, passed_along(): return lax.ppermute(value, axis, pairs)  9.07 us
    reduce_sum x1, other arithmetic, weighted(): jnp.sum(combined * weights)  4.28 us
  transfers between devices with their start and end apart: 13, of which 8 were waited for; matrix products, arithmetic and copies ran while one was open for 2% of the time, Pallas kernels for 0%

commit v1 on v0

v1 whole, which is shorter than its diff:
```python
import functools

import jax
import jax.numpy as jnp
from jax import lax
from jax.experimental import pallas as pl
from jax.experimental.pallas import tpu as pltpu
from jax.sharding import PartitionSpec as P


LINES = ("inst", "shard")
LANES = 128
SUBLANES = 8
PERIOD = 101
FACTOR = 37
WIDTH = 8


def tiled(stacked):
    columns = stacked.shape[2]
    return stacked.reshape(2, columns // LANES, LANES).transpose(1, 0, 2).reshape(2 * columns // LANES, LANES)


def untiled(flat):
    height = flat.shape[0]
    return flat.reshape(height // 2, 2, LANES).transpose(1, 0, 2).reshape(1, 2, height // 2 * LANES)


def split_kernel(columns, table, healthy, master, first, second, *outs):
    own, sums = outs[:6], outs[6]
    shard = lax.axis_index("shard")
    height = columns // LANES
    stride = SUBLANES * LANES
    present = healthy[shard] == lax.axis_index("inst")
    scale = jnp.where(present, 1.0, 0.0) / (2.0 * columns * PERIOD)
    place = (lax.broadcasted_iota(jnp.int32, (SUBLANES, LANES), 0) * LANES
             + lax.broadcasted_iota(jnp.int32, (SUBLANES, LANES), 1)) % PERIOD
    jump = float(FACTOR * (stride % PERIOD) % PERIOD)
    total = jnp.zeros((SUBLANES, LANES), jnp.float32)
    alone = jnp.zeros((SUBLANES, LANES), jnp.float32)
    for row in range(2):
        residue = table[2 * shard + row] * (columns % PERIOD) % PERIOD
        key = ((place + residue) % PERIOD * FACTOR % PERIOD + 1).astype(jnp.float32)

        def step(block, carry):
            key, total, alone = carry
            here = pl.ds(block * 2 * SUBLANES + row, SUBLANES, stride=2)
            there = pl.ds(block * SUBLANES, SUBLANES)
            m, f, s = master[here, :], first[here, :], second[here, :]
            own[row][there, :] = m
            own[2 + row][there, :] = f
            own[4 + row][there, :] = s
            total = total + (m + f + s) * key
            alone = alone + m * key
            key = key + jump
            return jnp.where(key > float(PERIOD), key - float(PERIOD), key), total, alone

        _, total, alone = lax.fori_loop(0, height // SUBLANES, step, (key, total, alone), unroll=4)
    sums[0:SUBLANES, :] = jnp.broadcast_to(jnp.sum(total) * scale, (SUBLANES, LANES))
    sums[SUBLANES:, :] = jnp.broadcast_to(jnp.sum(alone) * scale, (SUBLANES, LANES))


def split(arrays, table, healthy):
    columns = arrays[0].shape[2]
    height = columns // LANES
    piece = jax.ShapeDtypeStruct((height, LANES), jnp.float32)
    smem = pl.BlockSpec(memory_space=pltpu.SMEM)
    vmem = pl.BlockSpec(memory_space=pltpu.VMEM)
    outs = pl.pallas_call(
        functools.partial(split_kernel, columns),
        out_shape=[piece] * 6 + [jax.ShapeDtypeStruct((2 * SUBLANES, LANES), jnp.float32)],
        in_specs=[smem, smem, vmem, vmem, vmem],
        out_specs=[vmem] * 7,
        compiler_params=pltpu.CompilerParams(vmem_limit_bytes=8 * 1024 * 1024),
        name="split",
    )(table, healthy, *[tiled(a) for a in arrays])
    return outs[:6], outs[6]


def join_kernel(*refs):
    ins, outs = refs[:12], refs[12:]
    inst = lax.axis_index("inst")
    outer = (inst == 0) | (inst == lax.axis_size("inst") - 1)

    def fill(side):
        for array in range(3):
            height = ins[0].shape[0]

            def step(block, _):
                there = pl.ds(block * SUBLANES, SUBLANES)
                for row in range(2):
                    value = ins[side * 6 + array * 2 + 1 - row][there, :]
                    outs[array][pl.ds(block * 2 * SUBLANES + row, SUBLANES, stride=2), :] = value
                if array == 0:
                    whole = pl.ds(block * 2 * SUBLANES, 2 * SUBLANES)
                    outs[3][whole, :] = outs[0][whole, :].astype(jnp.bfloat16)
                return 0

            lax.fori_loop(0, height // SUBLANES, step, 0, unroll=4)

    pl.when(outer)(lambda: fill(0))
    pl.when(jnp.logical_not(outer))(lambda: fill(1))


def join(edge, here):
    height = edge[0].shape[0]
    vmem = pl.BlockSpec(memory_space=pltpu.VMEM)
    outs = pl.pallas_call(
        join_kernel,
        out_shape=[jax.ShapeDtypeStruct((2 * height, LANES), jnp.float32)] * 3
        + [jax.ShapeDtypeStruct((2 * height, LANES), jnp.bfloat16)],
        in_specs=[vmem] * 12,
        out_specs=[vmem] * 4,
        compiler_params=pltpu.CompilerParams(vmem_limit_bytes=8 * 1024 * 1024),
        name="join",
    )(*edge, *here)
    return tuple(untiled(v) for v in outs)


def hop(value, pairs):
    return lax.ppermute(value, LINES, pairs)


def restore(own, sums, source, instances, owners, turn):
    inst = lax.axis_index("inst")
    last = instances - 1
    mid = instances // 2

    def pairs(moves, filler=()):
        out = [(a * owners + s, b * owners + (s + d) % owners) for a, b, d in moves for s in range(owners)]
        return out + [(a * owners + s, a * owners + (s ^ 1)) for a in filler for s in range(owners)]

    across = pairs([(1, 2, 0), (2, 1, 0)], (0, 3))

    def turned(d):
        return pairs([(1, 1, d), (2, 2, d)], (0, 3))

    def shuttle(d):
        return pairs([(0, 1, 0), (3, 2, 0), (1, 0, d), (2, 3, d)])

    outer = (inst == 0) | (inst == last)
    mine_here = source == inst
    same_half = (source < mid) == (inst < mid)

    steps = [(1 << b, "shard", owners) for b in range((owners - 1).bit_length())]
    steps += [(1 << b, "inst", instances) for b in range((instances - 1).bit_length())]

    count = len(own)
    lag = 3
    got, far, near, full, edge, here = {}, {}, {}, {}, {}, {}

    def send_shuttle(t):
        cargo = own[min(t, count - 1)]
        shift = 0
        if t >= lag:
            cargo = jnp.where(outer, cargo, full[t - lag]) if t < count else full[t - lag]
            shift = turn + (t - lag) % 2
        back = hop(cargo, shuttle(shift))
        if t < count:
            got[t] = back
        if t >= lag:
            edge[t - lag] = back

    def tick(anchor):
        nonlocal sums
        if steps:
            step, axis, size = steps.pop(0)
            tied, _ = lax.optimization_barrier((sums, anchor))
            sums = tied + lax.ppermute(tied, axis, [(s, s ^ step) for s in range(size)])

    send_shuttle(0)
    send_shuttle(1)
    for t in range(count + 1):
        if t < count:
            near[t] = jnp.where(mine_here, own[t], got[t])
            far[t] = hop(near[t], across)
        if t >= 1:
            full[t - 1] = jnp.where(same_half, near[t - 1], far[t - 1])
        if t + 2 < count or t >= 1:
            send_shuttle(t + 2)
        if t >= 1:
            here[t - 1] = hop(full[t - 1], turned(turn + (t - 1) % 2))
        tick(near[t] if t < count else full[t - 1])
    while steps:
        tick(full[count - 1])
    return [edge[c] for c in range(count)], [here[c] for c in range(count)], sums


def on_device(master_old, first_old, second_old, healthy, slice_table):
    shard = lax.axis_index("shard")
    owners = lax.axis_size("shard")
    instances = lax.axis_size("inst")
    arrays = (master_old, first_old, second_old)
    turn = slice_table[0] // 2
    own, sums = split(arrays, slice_table, healthy)
    width = min(owners, WIDTH)
    step = width
    while step < owners:
        chosen = turn // step % 2 == 1
        moved = [lax.ppermute(v, "shard", [(s, (s + step) % owners) for s in range(owners)]) for v in own]
        own = [jnp.where(chosen, m, v) for m, v in zip(moved, own)]
        step *= 2
    begin = (shard - turn // width * width) % owners
    source = lax.dynamic_index_in_dim(healthy, begin, 0, keepdims=False)
    lowest = 1 if width == owners else 0

    def branch(turned_by):
        def run(pieces, terms, origin):
            return restore(pieces, terms, origin, instances, owners, turned_by)

        return run

    branches = [branch(t) for t in range(lowest, width)]
    edge, here, sums = lax.switch(turn % width - lowest, branches, own, sums, source)
    checksum = sums[::SUBLANES, 0].reshape(1, 2)
    return (*join(edge, here), checksum)


def solution(mesh):
    placed = (
        P("inst", "shard", None),
        P("inst", "shard", None),
        P("inst", "shard", None),
        P(),
        P(),
    )
    return jax.shard_map(
        on_device,
        mesh=mesh,
        in_specs=placed,
        out_specs=(
            P("inst", "shard", None),
            P("inst", "shard", None),
            P("inst", "shard", None),
            P("inst", "shard", None),
            P("inst", None),
        ),
        check_vma=False,
    )
```

time: 188 us -> 99.1 us (0.53)
  blocking collectives: 58.6 us -> 0 us
  waiting for transfers between devices: 85.5 us -> 42.2 us
  starting transfers between devices: 9.11 us -> 40.4 us
  between operations: 15 us -> 0.87 us
  other arithmetic: 12.4 us -> 0.45 us
  Pallas kernels: 0 us -> 4.53 us
    psum x1 -> x0, waiting for transfers between devices: 71.1 us -> none  [from_root(): return lax.psum(block, axis)]
    all_gather x3 -> x0, blocking collectives: 46.8 us -> none  [the longest x1 16.1 us: join_parts(): lax.all_gather(pieces[2], 'inst', axis=2, tiled=True)]
    ppermute x12 -> x26, starting transfers between devices: 9.07 us -> 40.4 us  [the longest x21 26.9 us: hop(): return lax.ppermute(value, LINES, pairs)]
    ppermute x12 -> x26, waiting for transfers between devices: 14.4 us -> 42.2 us  [the longest x21 34.6 us: hop(): return lax.ppermute(value, LINES, pairs)]
    psum x1 -> x0, blocking collectives: 11.8 us -> none  [grand_total(): return lax.psum(partial_value, 'shard')]
    select_n x12, other arithmetic: 4.98 us -> 0.4 us  [the longest x6 0.18 us: restore(): near[t] = jnp.where(mine_here, own[t], got[t])]
    pallas_call x0 -> x2, Pallas kernels: none -> 4.53 us  [the longest x1 3.42 us: join(): pl.pallas_call(join_kernel, out_shape=[jax.ShapeDtypeStruct((2 * height,...]
    reduce_sum x1 -> x0, other arithmetic: 4.28 us -> none  [weighted(): jnp.sum(combined * weights)]
  transfers between devices with their start and end apart: 13 -> 26, of which waited for: 8 -> 12; matrix products, arithmetic and copies ran while one was open for 2% -> 1% of each run, Pallas kernels for 0% -> 0%
where the time goes in v1:
time: 99.1 us; the launch traced here: 98 us
  waiting for transfers between devices  42.2 us (43%)
  starting transfers between devices  40.4 us (41%)
  local copies, waits for them, and re-layouts  7.7 us (8%)
  Pallas kernels  4.53 us (5%)
  loops' own time  1.74 us (2%)
    ppermute x21, waiting for transfers between devices, hop(): return lax.ppermute(value, LINES, pairs)  34.6 us
    ppermute x21, starting transfers between devices, hop(): return lax.ppermute(value, LINES, pairs)  26.9 us
    ppermute x5, starting transfers between devices, tick(): sums = tied + lax.ppermute(tied, axis, [(s, s ^ step) for s in range(size)])  13.5 us
    ppermute x5, waiting for transfers between devices, tick(): sums = tied + lax.ppermute(tied, axis, [(s, s ^ step) for s in range(size)])  7.61 us
    unnamed x12, local copies, waits for them, and re-layouts  4.93 us
    pallas_call x1, Pallas kernels, join(): pl.pallas_call(join_kernel, out_shape=[jax.ShapeDtypeStruct((2 * height,...  3.42 us
    cond x6, local copies, waits for them, and re-layouts  2 us
  transfers between devices with their start and end apart: 26, of which 12 were waited for; matrix products, arithmetic and copies ran while one was open for 1% of the time, Pallas kernels for 0%

profile of v1, /device:TPU:0, one launch (start us, length us, event | category | flops | bytes accessed | tf_op | source)
XLA Modules:
  0.0 98.0 jit_solution(14022745951568661595)
XLA Ops:
  0.6 0.6 copy-done.3
  1.5 0.6 copy-done.25
  2.2 1.0 %copy-done = f32[1,2,65536]{2,1,0:T(2,128)S(1)} copy-done((f32[1,2,65536]{2,1,0:T(2,128)S(1)}, f32[1,2,65536]{2,1,0:T(2,128)}, u32[]{:S(2)}) %copy-start) | copy-done | bytes 524312
  3.2 1.0 %copy-done.1 = f32[1,2,65536]{2,1,0:T(2,128)S(1)} copy-done((f32[1,2,65536]{2,1,0:T(2,128)S(1)}, f32[1,2,65536]{2,1,0:T(2,128)}, u32[]{:S(2)}) %copy-start.1) | copy-done | bytes 524312
  4.2 1.0 %copy-done.2 = f32[1,2,65536]{2,1,0:T(2,128)S(1)} copy-done((f32[1,2,65536]{2,1,0:T(2,128)S(1)}, f32[1,2,65536]{2,1,0:T(2,128)}, u32[]{:S(2)}) %copy-start.2) | copy-done | bytes 524312
  5.3 1.1 %split.1 = (f32[512,128]{1,0:T(8,128)S(1)}, f32[512,128]{1,0:T(8,128)S(1)}, f32[512,128]{1,0:T(8,128)S(1)}, f32[512,128]{1,0:T(8,128)S(1)}, f32[512,128]{1,0:T(8...) custom-call(s32[16]{0:T(128)S(1)} %copy-done.3, s32[8]{0:T(128)S(1)} %copy-done.25, f32[1024,128]{1,0:T(8,128)S(1)} %bitcast.51, ...), custom_call_target="tpu_custom_call" | custom-call | tf_op jit(solution)/shard_map/split/pallas_call | solution.py:69
  6.4 87.7 %conditional.1 = (f32[512,128]{1,0:T(8,128)}, f32[512,128]{1,0:T(8,128)}, f32[512,128]{1,0:T(8,128)}, f32[512,128]{1,0:T(8,128)}, f32[512,128]{1,0:T(8,128)}, /*...) conditional(s32[]{:T(128)} %clamp.3, (s32[]{:T(128)}, ...), branch_computations={%region_0.1_spmd, %region_1.2_spmd, %region_2.3_spmd, %region_3.4_... | conditional | flops 993293 | bytes 36480360 | solution.py:214
  6.7 3.1 %collective-permute-start.136 = (f32[512,128]{1,0:T(8,128)S(1)}, f32[512,128]{1,0:T(8,128)S(1)}, u32[]{:S(2)}, u32[]{:S(2)}) collective-permute-start(f32[512,128]{1,0:T(8,128)S(1)} %get-tuple-element.267), channel_id=1, source_target_pairs={{0,8},{1,9},{2,10},{3,11},{4,12},{5,13},{6,14},{7,15},{24,16},{25,... | collective-permute-start | bytes 786440 | tf_op jit(solution)/shard_map/cond/branch_5_fun/ppermute | solution.py:121
  9.8 0.1 collective-permute-start.130
  9.9 1.9 %collective-permute-start.133 = (f32[512,128]{1,0:T(8,128)S(1)}, f32[512,128]{1,0:T(8,128)S(1)}, u32[]{:S(2)}, u32[]{:S(2)}) collective-permute-start(f32[512,128]{1,0:T(8,128)S(1)} %get-tuple-element.265), channel_id=1, source_target_pairs={{0,8},{1,9},{2,10},{3,11},{4,12},{5,13},{6,14},{7,15},{24,16},{25,... | collective-permute-start | bytes 786440 | tf_op jit(solution)/shard_map/cond/branch_5_fun/ppermute | solution.py:121
  11.8 0.1 copy.18
  11.9 0.6 dynamic_slice.21
  13.1 3.8 %collective-permute-done.136 = f32[512,128]{1,0:T(8,128)S(1)} collective-permute-done((f32[512,128]{1,0:T(8,128)S(1)}, f32[512,128]{1,0:T(8,128)S(1)}, u32[]{:S(2)}, u32[]{:S(2)}) %collective-permute-start.136) | collective-permute-done | bytes 262176 | tf_op jit(solution)/shard_map/cond/branch_5_fun/ppermute | solution.py:121
  17.0 0.1 collective-permute-start.137
  17.0 5.5 %collective-permute-done.130 = f32[512,128]{1,0:T(8,128)S(1)} collective-permute-done((f32[512,128]{1,0:T(8,128)S(1)}, f32[512,128]{1,0:T(8,128)S(1)}, u32[]{:S(2)}, u32[]{:S(2)}) %collective-permute-start.130) | collective-permute-done | bytes 262176 | tf_op jit(solution)/shard_map/cond/branch_5_fun/ppermute | solution.py:121
  22.6 0.1 collective-permute-start.151
  22.7 4.7 %collective-permute-done.133 = f32[512,128]{1,0:T(8,128)S(1)} collective-permute-done((f32[512,128]{1,0:T(8,128)S(1)}, f32[512,128]{1,0:T(8,128)S(1)}, u32[]{:S(2)}, u32[]{:S(2)}) %collective-permute-start.133) | collective-permute-done | bytes 262176 | tf_op jit(solution)/shard_map/cond/branch_5_fun/ppermute | solution.py:121
  27.4 0.0 collective-permute-done.151
  27.4 1.7 %collective-permute-start.152 = (f32[16,128]{0,1:T(8,128)S(1)}, f32[16,128]{0,1:T(8,128)S(1)}, u32[]{:S(2)}, u32[]{:S(2)}) collective-permute-start(f32[16,128]{0,1:T(8,128)S(1)} %add.125), channel_id=1, source_target_pairs={{0,2},{1,3},{2,0},{3,1},{4,6},{5,7},{6,4},{7,5},{8,10},{9,11},{10,... | collective-permute-start | bytes 24584 | tf_op jit(solution)/shard_map/cond/branch_5_fun/ppermute | solution.py:169
  29.1 2.6 %collective-permute-done.152 = f32[16,128]{0,1:T(8,128)S(1)} collective-permute-done((f32[16,128]{0,1:T(8,128)S(1)}, f32[16,128]{0,1:T(8,128)S(1)}, u32[]{:S(2)}, u32[]{:S(2)}) %collective-permute-start.152) | collective-permute-done | bytes 8224 | tf_op jit(solution)/shard_map/cond/branch_5_fun/ppermute | solution.py:169
  31.7 1.7 %collective-permute-start.153 = (f32[16,128]{0,1:T(8,128)S(1)}, f32[16,128]{0,1:T(8,128)S(1)}, u32[]{:S(2)}, u32[]{:S(2)}) collective-permute-start(f32[16,128]{0,1:T(8,128)S(1)} %add.126), channel_id=1, source_target_pairs={{0,4},{1,5},{2,6},{3,7},{4,0},{5,1},{6,2},{7,3},{8,12},{9,13},{10,... | collective-permute-start | bytes 24584 | tf_op jit(solution)/shard_map/cond/branch_5_fun/ppermute | solution.py:169
  33.5 0.0 collective-permute-start.134
  34.1 0.6 collective-permute-start.131
  34.7 1.3 %collective-permute-done.153 = f32[16,128]{0,1:T(8,128)S(1)} collective-permute-done((f32[16,128]{0,1:T(8,128)S(1)}, f32[16,128]{0,1:T(8,128)S(1)}, u32[]{:S(2)}, u32[]{:S(2)}) %collective-permute-start.153) | collective-permute-done | bytes 8224 | tf_op jit(solution)/shard_map/cond/branch_5_fun/ppermute | solution.py:169
  36.1 0.0 collective-permute-done.137
  36.1 1.8 %collective-permute-start.138 = (f32[512,128]{1,0:T(8,128)S(1)}, f32[512,128]{1,0:T(8,128)S(1)}, u32[]{:S(2)}, u32[]{:S(2)}) collective-permute-start(f32[512,128]{1,0:T(8,128)S(1)} %get-tuple-element.434), channel_id=1, source_target_pairs={{0,8},{1,9},{2,10},{3,11},{4,12},{5,13},{6,14},{7,15},{24,16},{25,... | collective-permute-start | bytes 786440 | tf_op jit(solution)/shard_map/cond/branch_5_fun/ppermute | solution.py:121
  37.9 0.0 collective-permute-done.134
  38.0 5.7 %collective-permute-start.135 = (f32[512,128]{1,0:T(8,128)S(1)}, f32[512,128]{1,0:T(8,128)S(1)}, u32[]{:S(2)}, u32[]{:S(2)}) collective-permute-start(f32[512,128]{1,0:T(8,128)S(1)} %get-tuple-element.436), channel_id=1, source_target_pairs={{0,8},{1,9},{2,10},{3,11},{4,12},{5,13},{6,14},{7,15},{24,16},{25,... | collective-permute-start | bytes 786440 | tf_op jit(solution)/shard_map/cond/branch_5_fun/ppermute | solution.py:121
  43.7 0.0 collective-permute-done.131
  43.8 2.7 %collective-permute-start.132 = (f32[512,128]{1,0:T(8,128)S(1)}, f32[512,128]{1,0:T(8,128)S(1)}, u32[]{:S(2)}, u32[]{:S(2)}) collective-permute-start(f32[512,128]{1,0:T(8,128)S(1)} %get-tuple-element.438), channel_id=1, source_target_pairs={{0,8},{1,9},{2,10},{3,11},{4,12},{5,13},{6,14},{7,15},{24,16},{25,... | collective-permute-start | bytes 786440 | tf_op jit(solution)/shard_map/cond/branch_5_fun/ppermute | solution.py:121
  46.5 0.0 collective-permute-done.138
  46.6 0.7 copy-done.9
  47.2 0.0 collective-permute-start.143
  47.2 2.1 %collective-permute-done.135 = f32[512,128]{1,0:T(8,128)S(1)} collective-permute-done((f32[512,128]{1,0:T(8,128)S(1)}, f32[512,128]{1,0:T(8,128)S(1)}, u32[]{:S(2)}, u32[]{:S(2)}) %collective-permute-start.135) | collective-permute-done | bytes 262176 | tf_op jit(solution)/shard_map/cond/branch_5_fun/ppermute | solution.py:121
  49.4 0.7 copy-done.16
  50.1 2.3 %collective-permute-start.141 = (f32[512,128]{1,0:T(8,128)S(1)}, f32[512,128]{1,0:T(8,128)S(1)}, u32[]{:S(2)}, u32[]{:S(2)}) collective-permute-start(f32[512,128]{1,0:T(8,128)S(1)} %broadcast_select_fusion.76), channel_id=1, source_target_pairs={{8,16},{9,17},{10,18},{11,19},{12,20},{13,21},{14,22},{15,23},{16,... | collective-permute-start | bytes 786440 | tf_op jit(solution)/shard_map/cond/branch_5_fun/ppermute | solution.py:121
  52.3 2.9 %collective-permute-done.132 = f32[512,128]{1,0:T(8,128)S(1)} collective-permute-done((f32[512,128]{1,0:T(8,128)S(1)}, f32[512,128]{1,0:T(8,128)S(1)}, u32[]{:S(2)}, u32[]{:S(2)}) %collective-permute-start.132) | collective-permute-done | bytes 262176 | tf_op jit(solution)/shard_map/cond/branch_5_fun/ppermute | solution.py:121
  55.3 0.7 copy-done.23
  55.9 0.1 collective-permute-start.154
  56.0 0.0 collective-permute-start.147
  56.0 0.5 collective-permute-start.146
  56.5 3.7 %collective-permute-done.154 = f32[16,128]{0,1:T(8,128)S(1)} collective-permute-done((f32[16,128]{0,1:T(8,128)S(1)}, f32[16,128]{0,1:T(8,128)S(1)}, u32[]{:S(2)}, u32[]{:S(2)}) %collective-permute-start.154) | collective-permute-done | bytes 8224 | tf_op jit(solution)/shard_map/cond/branch_5_fun/ppermute | solution.py:169
  60.2 0.0 collective-permute-start.145
  60.2 0.0 collective-permute-done.143
  60.2 0.6 collective-permute-start.139
  60.8 0.0 collective-permute-done.141
  60.8 0.1 collective-permute-start.150
  60.9 1.2 %collective-permute-done.139 = f32[512,128]{1,0:T(8,128)S(1)} collective-permute-done((f32[512,128]{1,0:T(8,128)S(1)}, f32[512,128]{1,0:T(8,128)S(1)}, u32[]{:S(2)}, u32[]{:S(2)}) %collective-permute-start.139) | collective-permute-done | bytes 262176 | tf_op jit(solution)/shard_map/cond/branch_5_fun/ppermute | solution.py:121
  62.1 9.8 %collective-permute-start.155 = (f32[16,128]{0,1:T(8,128)S(1)}, f32[16,128]{0,1:T(8,128)S(1)}, u32[]{:S(2)}, u32[]{:S(2)}) collective-permute-start(f32[16,128]{0,1:T(8,128)S(1)} %add.128), channel_id=1, source_target_pairs={{0,16},{8,24},{16,0},{24,8},{1,17},{9,25},{17,1},{25,9},{2,18},{10... | collective-permute-start | bytes 24584 | tf_op jit(solution)/shard_map/cond/branch_5_fun/ppermute | solution.py:169
  72.0 0.0 collective-permute-done.147
  72.0 2.8 %collective-permute-start.144 = (f32[512,128]{1,0:T(8,128)S(1)}, f32[512,128]{1,0:T(8,128)}, u32[]{:S(2)}, u32[]{:S(2)}) collective-permute-start(f32[512,128]{1,0:T(8,128)S(1)} %broadcast_select_fusion.81), channel_id=1, source_target_pairs={{0,8},{1,9},{2,10},{3,11},{4,12},{5,13},{6,14},{7,15},{24,16},{25,... | collective-permute-start | bytes 786440 | tf_op jit(solution)/shard_map/cond/branch_5_fun/ppermute | solution.py:121
  74.8 0.0 collective-permute-done.146
  74.8 0.4 collective-permute-start.149
  75.2 0.0 collective-permute-done.145
  75.2 3.9 %collective-permute-start.142 = (f32[512,128]{1,0:T(8,128)S(1)}, f32[512,128]{1,0:T(8,128)}, u32[]{:S(2)}, u32[]{:S(2)}) collective-permute-start(f32[512,128]{1,0:T(8,128)S(1)} %broadcast_select_fusion.82), channel_id=1, source_target_pairs={{0,8},{1,9},{2,10},{3,11},{4,12},{5,13},{6,14},{7,15},{24,16},{25,... | collective-permute-start | bytes 786440 | tf_op jit(solution)/shard_map/cond/branch_5_fun/ppermute | solution.py:121
  79.1 0.0 collective-permute-done.155
  79.1 0.4 collective-permute-start.140
  79.5 0.1 slice.22
  79.6 3.2 %collective-permute-done.144 = f32[512,128]{1,0:T(8,128)} collective-permute-done((f32[512,128]{1,0:T(8,128)S(1)}, f32[512,128]{1,0:T(8,128)}, u32[]{:S(2)}, u32[]{:S(2)}) %collective-permute-start.144) | collective-permute-done | bytes 262176 | tf_op jit(solution)/shard_map/cond/branch_5_fun/ppermute | solution.py:121
  82.8 0.0 collective-permute-done.149
  82.8 7.7 %collective-permute-done.142 = f32[512,128]{1,0:T(8,128)} collective-permute-done((f32[512,128]{1,0:T(8,128)S(1)}, f32[512,128]{1,0:T(8,128)}, u32[]{:S(2)}, u32[]{:S(2)}) %collective-permute-start.142) | collective-permute-done | bytes 262176 | tf_op jit(solution)/shard_map/cond/branch_5_fun/ppermute | solution.py:121
  90.5 3.6 %collective-permute-done.140 = f32[512,128]{1,0:T(8,128)} collective-permute-done((f32[512,128]{1,0:T(8,128)S(1)}, f32[512,128]{1,0:T(8,128)}, u32[]{:S(2)}, u32[]{:S(2)}) %collective-permute-start.140) | collective-permute-done | bytes 262176 | tf_op jit(solution)/shard_map/cond/branch_5_fun/ppermute | solution.py:121
  94.1 0.5 copy-done.26
  94.6 3.4 %join.1 = (f32[1024,128]{1,0:T(8,128)}, f32[1024,128]{1,0:T(8,128)}, f32[1024,128]{1,0:T(8,128)}, bf16[1024,128]{1,0:T(8,128)(2,1)}) custom-call(f32[512,128]{1,0:T(8,128)} %get-tuple-element.324.refs_0_, f32[512,128]{1,0:T(8,128)} %get-tuple-element.325.refs_1_, f32[512,128]{1,0:T(8,128)} %get-tuple-element.326.refs_2_, ...), custom_call_target="tpu_custom_call" | custom-call | tf_op jit(solution)/shard_map/join/pallas_call | solution.py:108
  (29 shorter events, 0.5 us)
Async XLA Ops:
  0.6 0.7 copy-start.3
  1.5 0.7 copy-start.25
  2.2 1.0 %copy-start = (f32[1,2,65536]{2,1,0:T(2,128)S(1)}, f32[1,2,65536]{2,1,0:T(2,128)}, u32[]{:S(2)}) copy-start(f32[1,2,65536]{2,1,0:T(2,128)} %param.12) | copy-start | bytes 1572868
  3.2 1.0 %copy-start.1 = (f32[1,2,65536]{2,1,0:T(2,128)S(1)}, f32[1,2,65536]{2,1,0:T(2,128)}, u32[]{:S(2)}) copy-start(f32[1,2,65536]{2,1,0:T(2,128)} %param.13) | copy-start | bytes 1572868
  4.2 1.0 %copy-start.2 = (f32[1,2,65536]{2,1,0:T(2,128)S(1)}, f32[1,2,65536]{2,1,0:T(2,128)}, u32[]{:S(2)}) copy-start(f32[1,2,65536]{2,1,0:T(2,128)} %param.14) | copy-start | bytes 1572868
  6.7 10.3 %collective-permute-start.136 = (f32[512,128]{1,0:T(8,128)S(1)}, f32[512,128]{1,0:T(8,128)S(1)}, u32[]{:S(2)}, u32[]{:S(2)}) collective-permute-start(f32[512,128]{1,0:T(8,128)S(1)} %get-tuple-element.267), channel_id=1, source_target_pairs={{0,8},{1,9},{2,10},{3,11},{4,12},{5,13},{6,14},{7,15},{24,16},{25,... | collective-permute-start | bytes 786440 | tf_op jit(solution)/shard_map/cond/branch_5_fun/ppermute | solution.py:121
  9.8 12.8 %collective-permute-start.130 = (f32[512,128]{1,0:T(8,128)S(1)}, f32[512,128]{1,0:T(8,128)S(1)}, u32[]{:S(2)}, u32[]{:S(2)}) collective-permute-start(f32[512,128]{1,0:T(8,128)S(1)} %get-tuple-element.263), channel_id=1, source_target_pairs={{0,8},{1,9},{2,10},{3,11},{4,12},{5,13},{6,14},{7,15},{24,16},{25,... | collective-permute-start | bytes 786440 | tf_op jit(solution)/shard_map/cond/branch_5_fun/ppermute | solution.py:121
  9.9 17.5 %collective-permute-start.133 = (f32[512,128]{1,0:T(8,128)S(1)}, f32[512,128]{1,0:T(8,128)S(1)}, u32[]{:S(2)}, u32[]{:S(2)}) collective-permute-start(f32[512,128]{1,0:T(8,128)S(1)} %get-tuple-element.265), channel_id=1, source_target_pairs={{0,8},{1,9},{2,10},{3,11},{4,12},{5,13},{6,14},{7,15},{24,16},{25,... | collective-permute-start | bytes 786440 | tf_op jit(solution)/shard_map/cond/branch_5_fun/ppermute | solution.py:121
  17.0 19.1 %collective-permute-start.137 = (f32[512,128]{1,0:T(8,128)S(1)}, f32[512,128]{1,0:T(8,128)S(1)}, u32[]{:S(2)}, u32[]{:S(2)}) collective-permute-start(f32[512,128]{1,0:T(8,128)S(1)} %broadcast_select_fusion.78), channel_id=1, source_target_pairs={{8,16},{9,17},{10,18},{11,19},{12,20},{13,21},{14,22},{15,23},{16,... | collective-permute-start | bytes 786440 | tf_op jit(solution)/shard_map/cond/branch_5_fun/ppermute | solution.py:121
  22.6 4.8 %collective-permute-start.151 = (f32[16,128]{0,1:T(8,128)S(1)}, f32[16,128]{0,1:T(8,128)S(1)}, u32[]{:S(2)}, u32[]{:S(2)}) collective-permute-start(f32[16,128]{0,1:T(8,128)S(1)} %copy.18), channel_id=1, source_target_pairs={{0,1},{1,0},{2,3},{3,2},{4,5},{5,4},{6,7},{7,6},{8,9},{9,8},{10,11... | collective-permute-start | bytes 24584 | tf_op jit(solution)/shard_map/cond/branch_5_fun/ppermute | solution.py:169
  27.4 4.3 %collective-permute-start.152 = (f32[16,128]{0,1:T(8,128)S(1)}, f32[16,128]{0,1:T(8,128)S(1)}, u32[]{:S(2)}, u32[]{:S(2)}) collective-permute-start(f32[16,128]{0,1:T(8,128)S(1)} %add.125), channel_id=1, source_target_pairs={{0,2},{1,3},{2,0},{3,1},{4,6},{5,7},{6,4},{7,5},{8,10},{9,11},{10,... | collective-permute-start | bytes 24584 | tf_op jit(solution)/shard_map/cond/branch_5_fun/ppermute | solution.py:169
  31.7 4.3 %collective-permute-start.153 = (f32[16,128]{0,1:T(8,128)S(1)}, f32[16,128]{0,1:T(8,128)S(1)}, u32[]{:S(2)}, u32[]{:S(2)}) collective-permute-start(f32[16,128]{0,1:T(8,128)S(1)} %add.126), channel_id=1, source_target_pairs={{0,4},{1,5},{2,6},{3,7},{4,0},{5,1},{6,2},{7,3},{8,12},{9,13},{10,... | collective-permute-start | bytes 24584 | tf_op jit(solution)/shard_map/cond/branch_5_fun/ppermute | solution.py:169
  33.5 4.5 %collective-permute-start.134 = (f32[512,128]{1,0:T(8,128)S(1)}, f32[512,128]{1,0:T(8,128)S(1)}, u32[]{:S(2)}, u32[]{:S(2)}) collective-permute-start(f32[512,128]{1,0:T(8,128)S(1)} %broadcast_select_fusion.79), channel_id=1, source_target_pairs={{8,16},{9,17},{10,18},{11,19},{12,20},{13,21},{14,22},{15,23},{16,... | collective-permute-start | bytes 786440 | tf_op jit(solution)/shard_map/cond/branch_5_fun/ppermute | solution.py:121
  34.1 9.6 %collective-permute-start.131 = (f32[512,128]{1,0:T(8,128)S(1)}, f32[512,128]{1,0:T(8,128)S(1)}, u32[]{:S(2)}, u32[]{:S(2)}) collective-permute-start(f32[512,128]{1,0:T(8,128)S(1)} %broadcast_select_fusion.80), channel_id=1, source_target_pairs={{8,16},{9,17},{10,18},{11,19},{12,20},{13,21},{14,22},{15,23},{16,... | collective-permute-start | bytes 786440 | tf_op jit(solution)/shard_map/cond/branch_5_fun/ppermute | solution.py:121
  36.1 10.4 %collective-permute-start.138 = (f32[512,128]{1,0:T(8,128)S(1)}, f32[512,128]{1,0:T(8,128)S(1)}, u32[]{:S(2)}, u32[]{:S(2)}) collective-permute-start(f32[512,128]{1,0:T(8,128)S(1)} %get-tuple-element.434), channel_id=1, source_target_pairs={{0,8},{1,9},{2,10},{3,11},{4,12},{5,13},{6,14},{7,15},{24,16},{25,... | collective-permute-start | bytes 786440 | tf_op jit(solution)/shard_map/cond/branch_5_fun/ppermute | solution.py:121
  38.0 11.4 %collective-permute-start.135 = (f32[512,128]{1,0:T(8,128)S(1)}, f32[512,128]{1,0:T(8,128)S(1)}, u32[]{:S(2)}, u32[]{:S(2)}) collective-permute-start(f32[512,128]{1,0:T(8,128)S(1)} %get-tuple-element.436), channel_id=1, source_target_pairs={{0,8},{1,9},{2,10},{3,11},{4,12},{5,13},{6,14},{7,15},{24,16},{25,... | collective-permute-start | bytes 786440 | tf_op jit(solution)/shard_map/cond/branch_5_fun/ppermute | solution.py:121
  43.8 11.4 %collective-permute-start.132 = (f32[512,128]{1,0:T(8,128)S(1)}, f32[512,128]{1,0:T(8,128)S(1)}, u32[]{:S(2)}, u32[]{:S(2)}) collective-permute-start(f32[512,128]{1,0:T(8,128)S(1)} %get-tuple-element.438), channel_id=1, source_target_pairs={{0,8},{1,9},{2,10},{3,11},{4,12},{5,13},{6,14},{7,15},{24,16},{25,... | collective-permute-start | bytes 786440 | tf_op jit(solution)/shard_map/cond/branch_5_fun/ppermute | solution.py:121
  46.5 0.7 copy-start.9
  47.2 13.0 %collective-permute-start.143 = (f32[512,128]{1,0:T(8,128)S(1)}, f32[512,128]{1,0:T(8,128)S(1)}, u32[]{:S(2)}, u32[]{:S(2)}) collective-permute-start(f32[512,128]{1,0:T(8,128)S(1)} %broadcast_select_fusion.75), channel_id=1, source_target_pairs={{8,16},{9,17},{10,18},{11,19},{12,20},{13,21},{14,22},{15,23},{16,... | collective-permute-start | bytes 786440 | tf_op jit(solution)/shard_map/cond/branch_5_fun/ppermute | solution.py:121
  49.4 0.7 copy-start.16
  50.1 10.8 %collective-permute-start.141 = (f32[512,128]{1,0:T(8,128)S(1)}, f32[512,128]{1,0:T(8,128)S(1)}, u32[]{:S(2)}, u32[]{:S(2)}) collective-permute-start(f32[512,128]{1,0:T(8,128)S(1)} %broadcast_select_fusion.76), channel_id=1, source_target_pairs={{8,16},{9,17},{10,18},{11,19},{12,20},{13,21},{14,22},{15,23},{16,... | collective-permute-start | bytes 786440 | tf_op jit(solution)/shard_map/cond/branch_5_fun/ppermute | solution.py:121
  55.2 0.7 copy-start.23
  55.9 4.3 %collective-permute-start.154 = (f32[16,128]{0,1:T(8,128)S(1)}, f32[16,128]{0,1:T(8,128)S(1)}, u32[]{:S(2)}, u32[]{:S(2)}) collective-permute-start(f32[16,128]{0,1:T(8,128)S(1)} %add.127), channel_id=1, source_target_pairs={{0,8},{8,0},{16,24},{24,16},{1,9},{9,1},{17,25},{25,17},{2,10},{10... | collective-permute-start | bytes 24584 | tf_op jit(solution)/shard_map/cond/branch_5_fun/ppermute | solution.py:169
  56.0 16.0 %collective-permute-start.147 = (f32[512,128]{1,0:T(8,128)S(1)}, f32[512,128]{1,0:T(8,128)}, u32[]{:S(2)}, u32[]{:S(2)}) collective-permute-start(f32[512,128]{1,0:T(8,128)S(1)} %get-tuple-element.435), channel_id=1, source_target_pairs={{8,14},{9,15},{10,8},{11,9},{12,10},{13,11},{14,12},{15,13},{16,22... | collective-permute-start | bytes 786440 | tf_op jit(solution)/shard_map/cond/branch_5_fun/ppermute | solution.py:121
  56.0 18.8 %collective-permute-start.146 = (f32[512,128]{1,0:T(8,128)S(1)}, f32[512,128]{1,0:T(8,128)}, u32[]{:S(2)}, u32[]{:S(2)}) collective-permute-start(f32[512,128]{1,0:T(8,128)S(1)} %get-tuple-element.437), channel_id=1, source_target_pairs={{8,15},{9,8},{10,9},{11,10},{12,11},{13,12},{14,13},{15,14},{16,23... | collective-permute-start | bytes 786440 | tf_op jit(solution)/shard_map/cond/branch_5_fun/ppermute | solution.py:121
  60.2 15.0 %collective-permute-start.145 = (f32[512,128]{1,0:T(8,128)S(1)}, f32[512,128]{1,0:T(8,128)}, u32[]{:S(2)}, u32[]{:S(2)}) collective-permute-start(f32[512,128]{1,0:T(8,128)S(1)} %get-tuple-element.439), channel_id=1, source_target_pairs={{8,14},{9,15},{10,8},{11,9},{12,10},{13,11},{14,12},{15,13},{16,22... | collective-permute-start | bytes 786440 | tf_op jit(solution)/shard_map/cond/branch_5_fun/ppermute | solution.py:121
  60.2 1.9 %collective-permute-start.139 = (f32[512,128]{1,0:T(8,128)S(1)}, f32[512,128]{1,0:T(8,128)S(1)}, u32[]{:S(2)}, u32[]{:S(2)}) collective-permute-start(f32[512,128]{1,0:T(8,128)S(1)} %broadcast_select_fusion.77), channel_id=1, source_target_pairs={{8,16},{9,17},{10,18},{11,19},{12,20},{13,21},{14,22},{15,23},{16,... | collective-permute-start | bytes 786440 | tf_op jit(solution)/shard_map/cond/branch_5_fun/ppermute | solution.py:121
  60.8 18.2 %collective-permute-start.150 = (f32[512,128]{1,0:T(8,128)S(1)}, f32[512,128]{1,0:T(8,128)}, u32[]{:S(2)}, u32[]{:S(2)}) collective-permute-start(f32[512,128]{1,0:T(8,128)S(1)} %broadcast_select_fusion.81), channel_id=1, source_target_pairs={{8,15},{9,8},{10,9},{11,10},{12,11},{13,12},{14,13},{15,14},{16,23... | collective-permute-start | bytes 786440 | tf_op jit(solution)/shard_map/cond/branch_5_fun/ppermute | solution.py:121
  62.1 17.0 %collective-permute-start.155 = (f32[16,128]{0,1:T(8,128)S(1)}, f32[16,128]{0,1:T(8,128)S(1)}, u32[]{:S(2)}, u32[]{:S(2)}) collective-permute-start(f32[16,128]{0,1:T(8,128)S(1)} %add.128), channel_id=1, source_target_pairs={{0,16},{8,24},{16,0},{24,8},{1,17},{9,25},{17,1},{25,9},{2,18},{10... | collective-permute-start | bytes 24584 | tf_op jit(solution)/shard_map/cond/branch_5_fun/ppermute | solution.py:169
  72.0 10.8 %collective-permute-start.144 = (f32[512,128]{1,0:T(8,128)S(1)}, f32[512,128]{1,0:T(8,128)}, u32[]{:S(2)}, u32[]{:S(2)}) collective-permute-start(f32[512,128]{1,0:T(8,128)S(1)} %broadcast_select_fusion.81), channel_id=1, source_target_pairs={{0,8},{1,9},{2,10},{3,11},{4,12},{5,13},{6,14},{7,15},{24,16},{25,... | collective-permute-start | bytes 786440 | tf_op jit(solution)/shard_map/cond/branch_5_fun/ppermute | solution.py:121
  74.8 8.0 %collective-permute-start.149 = (f32[512,128]{1,0:T(8,128)S(1)}, f32[512,128]{1,0:T(8,128)}, u32[]{:S(2)}, u32[]{:S(2)}) collective-permute-start(f32[512,128]{1,0:T(8,128)S(1)} %broadcast_select_fusion.82), channel_id=1, source_target_pairs={{8,14},{9,15},{10,8},{11,9},{12,10},{13,11},{14,12},{15,13},{16,22... | collective-permute-start | bytes 786440 | tf_op jit(solution)/shard_map/cond/branch_5_fun/ppermute | solution.py:121
  75.2 15.3 %collective-permute-start.142 = (f32[512,128]{1,0:T(8,128)S(1)}, f32[512,128]{1,0:T(8,128)}, u32[]{:S(2)}, u32[]{:S(2)}) collective-permute-start(f32[512,128]{1,0:T(8,128)S(1)} %broadcast_select_fusion.82), channel_id=1, source_target_pairs={{0,8},{1,9},{2,10},{3,11},{4,12},{5,13},{6,14},{7,15},{24,16},{25,... | collective-permute-start | bytes 786440 | tf_op jit(solution)/shard_map/cond/branch_5_fun/ppermute | solution.py:121
  79.1 11.4 %collective-permute-start.148 = (f32[512,128]{1,0:T(8,128)S(1)}, f32[512,128]{1,0:T(8,128)}, u32[]{:S(2)}, u32[]{:S(2)}) collective-permute-start(f32[512,128]{1,0:T(8,128)S(1)} %broadcast_select_fusion.83), channel_id=1, source_target_pairs={{8,15},{9,8},{10,9},{11,10},{12,11},{13,12},{14,13},{15,14},{16,23... | collective-permute-start | bytes 786440 | tf_op jit(solution)/shard_map/cond/branch_5_fun/ppermute | solution.py:121
  79.1 15.0 %collective-permute-start.140 = (f32[512,128]{1,0:T(8,128)S(1)}, f32[512,128]{1,0:T(8,128)}, u32[]{:S(2)}, u32[]{:S(2)}) collective-permute-start(f32[512,128]{1,0:T(8,128)S(1)} %broadcast_select_fusion.83), channel_id=1, source_target_pairs={{0,8},{1,9},{2,10},{3,11},{4,12},{5,13},{6,14},{7,15},{24,16},{25,... | collective-permute-start | bytes 786440 | tf_op jit(solution)/shard_map/cond/branch_5_fun/ppermute | solution.py:121
  94.1 0.5 copy-start.26
